TPU v7x, 32 devices: a whole 2x2x4 slice. The times are simulated.
32 devices in a mesh: groups: 2 (over y), ulysses: 8 (over z, x), seq: 2 (over core).
Axes of the slice: x: 2, y: 2, z: 4, core: 2. Of those that a mesh axis runs over, the one named last changes fastest.
Arguments:
- query_states: bfloat16 [2048, 8192], P(('groups', 'ulysses', 'seq')), parts along dimension 0, may hold values from -6 to 6
- key_states: bfloat16 [2048, 1024], P(('groups', 'ulysses', 'seq')), parts along dimension 0, may hold values from -6 to 6
- value_states: bfloat16 [2048, 1024], P(('groups', 'ulysses', 'seq')), parts along dimension 0, may hold values from -6 to 6
- turn_ids: int32 [2048], P('groups'), parts along dimension 0, may hold values from 0 to 3, never falling along the last dimension, each value on 1 to 512 neighbouring positions
- judge_positions: int32 [256], P('groups'), parts along dimension 0, may hold values from 0 to 1023, as said below
Outputs:
- attended_states: bfloat16 [2048, 8192], P(('groups', 'ulysses', 'seq')), parts along dimension 0
There are 2 independent parts, one for each index of `groups`. A program takes and returns all parts, laid end to end along the dimension named above; each array names one. Nothing has to cross between parts.
Inputs may be any that keep to these rules, and one draw needn't show every extreme that they name: `turn_ids`: turn numbers never fall along the conversation; every turn spans 1 to 512 tokens, one exactly that many. `judge_positions`: distinct positions, 0 and 1023 among them.
All inputs are finite; a program needn't handle non-finite values.
Results may differ from a plain program's by a relative error of at most 0.004.
Values may be sent and summed in bfloat16 or wider, within the bound.
No kernel may reach another device: no remote copies, remote signals or barrier semaphores. Data moves between devices by JAX's collectives and lax.ppermute only.
A program may use at most 64 MiB of HBM per device.

v0:
```python
import math
import jax
import jax.numpy as jnp
from jax import lax
from jax.sharding import PartitionSpec as P

HEAD_DIM = 128
floor_score = -1e30


def absorb(
    carried,
    query_block,
    query_place,
    query_turn,
    keys_block,
    values_block,
    keys_place,
    keys_turn,
    keys_judge,
    scaling,
):
    maxima, totals, running = carried
    scores = (
        jnp.einsum("qhd,kd->qhk", query_block, keys_block, preferred_element_type=jnp.float32)
        * scaling
    )
    visible = (keys_place[None, :] <= query_place[:, None]) & (
        (keys_turn[None, :] == query_turn[:, None]) | keys_judge[None, :]
    )
    scores = jnp.where(visible[:, None, :], scores, floor_score)
    newest = jnp.maximum(maxima, jnp.max(scores, axis=2))
    factor = jnp.exp(maxima - newest)
    weights = jnp.exp(scores - newest[:, :, None])
    totals = totals * factor + jnp.sum(weights, axis=2)
    running = running * factor[:, :, None] + jnp.einsum(
        "qhk,kd->qhd",
        weights.astype(jnp.bfloat16),
        values_block,
        preferred_element_type=jnp.float32,
    )
    return (newest, totals, running)


def attend(
    carried,
    queries,
    query_place,
    query_turn,
    key_rows,
    value_rows,
    keys_place,
    keys_turn,
    keys_judge,
    scaling,
):
    query_count = queries.shape[0]
    key_count = key_rows.shape[0]
    query_step = math.gcd(query_count, 512)
    key_step = math.gcd(key_count, 512)

    def over_queries(row_index, totals_all):
        offset = row_index * query_step
        query_block = lax.dynamic_slice_in_dim(queries, offset, query_step, 0)
        block_place = lax.dynamic_slice_in_dim(query_place, offset, query_step, 0)
        block_turn = lax.dynamic_slice_in_dim(query_turn, offset, query_step, 0)
        window = tuple(
            (lax.dynamic_slice_in_dim(member, offset, query_step, 0) for member in totals_all)
        )

        def over_keys(key_index, current):
            key_offset = key_index * key_step
            keys_block = lax.dynamic_slice_in_dim(key_rows, key_offset, key_step, 0)
            values_block = lax.dynamic_slice_in_dim(value_rows, key_offset, key_step, 0)
            block_keys_place = lax.dynamic_slice_in_dim(keys_place, key_offset, key_step, 0)
            block_keys_turn = lax.dynamic_slice_in_dim(keys_turn, key_offset, key_step, 0)
            block_keys_judge = lax.dynamic_slice_in_dim(keys_judge, key_offset, key_step, 0)
            return lax.cond(
                jnp.max(block_place) >= jnp.min(block_keys_place),
                lambda inside: absorb(
                    inside,
                    query_block,
                    block_place,
                    block_turn,
                    keys_block,
                    values_block,
                    block_keys_place,
                    block_keys_turn,
                    block_keys_judge,
                    scaling,
                ),
                lambda inside: inside,
                current,
            )

        window = lax.fori_loop(0, key_count // key_step, over_keys, window)
        return tuple(
            (
                lax.dynamic_update_slice_in_dim(member, updated, offset, 0)
                for member, updated in zip(totals_all, window)
            )
        )

    return lax.fori_loop(0, query_count // query_step, over_queries, carried)


def spread(array, copies):
    row_count = array.shape[0]
    shared_heads = array.shape[1] // HEAD_DIM
    widened = jnp.broadcast_to(
        array.reshape(row_count, shared_heads, 1, HEAD_DIM),
        (row_count, shared_heads, copies // shared_heads, HEAD_DIM),
    )
    return widened.reshape(row_count, copies, HEAD_DIM)


def shards(query_states, key_states, value_states, turn_ids, judge_positions):
    tokens_here = query_states.shape[0]
    ulysses_count = lax.axis_size("ulysses")
    stripe_count = lax.axis_size("seq")
    stripe = lax.axis_index("seq")
    heads_here = query_states.shape[1] // HEAD_DIM // ulysses_count
    seq_total = tokens_here * ulysses_count * stripe_count
    scaling = 1.0 / math.sqrt(HEAD_DIM)
    positions = jnp.arange(seq_total, dtype=jnp.int32)
    judged = jnp.any(positions[:, None] == judge_positions[None, :], axis=1)
    exchanged = lax.all_to_all(
        query_states.reshape(tokens_here, ulysses_count, heads_here * HEAD_DIM),
        "ulysses",
        split_axis=1,
        concat_axis=0,
        tiled=True,
    )
    query_total = ulysses_count * tokens_here
    queries = exchanged.reshape(query_total, heads_here, HEAD_DIM)
    local_rows = jnp.arange(query_total, dtype=jnp.int32)
    query_place = (
        local_rows // tokens_here * stripe_count + stripe
    ) * tokens_here + local_rows % tokens_here
    query_turn = jnp.take(turn_ids, query_place)
    carried = (
        jnp.full((query_total, heads_here), floor_score, jnp.float32),
        jnp.zeros((query_total, heads_here), jnp.float32),
        jnp.zeros((query_total, heads_here, HEAD_DIM), jnp.float32),
    )
    keys_out, values_out = (
        lax.all_to_all(
            spread(key_states, ulysses_count), "ulysses", split_axis=1, concat_axis=0, tiled=True
        ),
        lax.all_to_all(
            spread(value_states, ulysses_count), "ulysses", split_axis=1, concat_axis=0, tiled=True
        ),
    )
    key_rows = keys_out.reshape(query_total, HEAD_DIM)
    value_rows = values_out.reshape(query_total, HEAD_DIM)
    pieces = (
        lax.all_gather(key_rows, "seq", axis=0, tiled=True),
        lax.all_gather(value_rows, "seq", axis=0, tiled=True),
    )
    piece_rows = pieces[0].shape[0]
    gathered_rows = jnp.arange(piece_rows, dtype=jnp.int32)
    source_stripe = gathered_rows // query_total
    within = gathered_rows % query_total
    key_place = (
        within // tokens_here * stripe_count + source_stripe
    ) * tokens_here + within % tokens_here
    maxima, totals, running = attend(
        carried,
        queries,
        query_place,
        query_turn,
        pieces[0],
        pieces[1],
        key_place,
        jnp.take(turn_ids, key_place),
        jnp.take(judged, key_place),
        scaling,
    )
    result = (
        (running / totals[:, :, None])
        .astype(jnp.bfloat16)
        .reshape(query_total, 1, heads_here * HEAD_DIM)
    )
    returned = lax.all_to_all(result, "ulysses", split_axis=0, concat_axis=1, tiled=True)
    return returned.reshape(tokens_here, ulysses_count * heads_here * HEAD_DIM)


def solution(mesh):
    placed = (
        P(("groups", "ulysses", "seq"), None),
        P(("groups", "ulysses", "seq"), None),
        P(("groups", "ulysses", "seq"), None),
        P("groups"),
        P("groups"),
    )
    return jax.shard_map(
        shards,
        mesh=mesh,
        in_specs=placed,
        out_specs=P(("groups", "ulysses", "seq"), None),
        check_vma=False,
    )
```

profile of v0, /device:TPU:0, one launch (start us, length us, event | category | flops | bytes accessed | tf_op | source)
XLA Modules:
  0.0 126.2 jit_solution(8405274671733121284)
XLA Ops:
  1.6 7.3 %all-to-all-start = ((bf16[64,8,128]{2,0,1:T(8,128)(2,1)}), bf16[64,8,128]{2,0,1:T(8,128)(2,1)S(1)}, u32[]{:S(2)}, u32[]{:S(2)}) async-start(bf16[64,8,128]{2,0,1:T(8,128)(2,1)} %copy_bitcast_fusion.2), calls=%async_computation | async-start | bytes 262144 | tf_op jit(solution)/shard_map/all_to_all | solution.py:147
  10.4 5.8 %all-to-all-done = bf16[64,8,128]{2,0,1:T(8,128)(2,1)S(1)} async-done(((bf16[64,8,128]{2,0,1:T(8,128)(2,1)}), bf16[64,8,128]{2,0,1:T(8,128)(2,1)S(1)}, u32[]{:S(2)}, u32[]{:S(2)}) %all-to-all-start) | async-done | bytes 131104 | tf_op jit(solution)/shard_map/all_to_all | solution.py:147
  16.2 3.4 %all-to-all-start.2 = ((bf16[64,8,128]{2,0,1:T(8,128)(2,1)}), bf16[64,8,128]{2,0,1:T(8,128)(2,1)S(1)}, u32[]{:S(2)}, u32[]{:S(2)}) async-start(bf16[64,8,128]{2,0,1:T(8,128)(2,1)} %copy_bitcast_fusion.1), calls=%async_computation.2 | async-start | bytes 262144 | tf_op jit(solution)/shard_map/all_to_all | solution.py:150
  19.6 2.3 %copy.51 = bf16[8,8,8,1024]{3,2,0,1:T(8,128)(2,1)} copy(bf16[8,8,8,1024]{3,2,1,0:T(8,128)(2,1)} %bitcast.71) | data formatting | bytes 2097152 | tf_op jit(solution)/shard_map/reshape | solution.py:128
  21.9 5.0 %all-to-all-done.2 = bf16[64,8,128]{2,0,1:T(8,128)(2,1)S(1)} async-done(((bf16[64,8,128]{2,0,1:T(8,128)(2,1)}), bf16[64,8,128]{2,0,1:T(8,128)(2,1)S(1)}, u32[]{:S(2)}, u32[]{:S(2)}) %all-to-all-start.2) | async-done | bytes 131104 | tf_op jit(solution)/shard_map/all_to_all | solution.py:150
  26.9 3.6 %all-to-all-start.1 = ((bf16[64,8,1024]{2,0,1:T(8,128)(2,1)}), bf16[64,8,1024]{2,0,1:T(8,128)(2,1)S(1)}, u32[]{:S(2)}, u32[]{:S(2)}) async-start(bf16[64,8,1024]{2,0,1:T(8,128)(2,1)} %bitcast.66), calls=%async_computation.1 | async-start | bytes 2097152 | tf_op jit(solution)/shard_map/all_to_all | solution.py:127
  30.5 5.7 %gather_fusion = s32[1024]{0:T(1024)S(1)} fusion(s32[1024]{0:T(1024)} %param.12, s32[1024]{0:T(1024)S(1)} %broadcast_clamp_fusion), kind=kCustom, calls=%fused_computation | custom fusion | bytes 12288 | tf_op jit(solution)/shard_map/jit(_take)/gather | solution.py:175
  36.3 2.3 %gather_fusion.1 = s32[512]{0:T(512)S(1)} fusion(s32[1024]{0:T(1024)S(1)} %copy-done.1, s32[1024]{0:T(1024)S(1)} %pad_clamp_fusion), kind=kCustom, calls=%fused_computation.1 | custom fusion | bytes 6144 | tf_op jit(solution)/shard_map/jit(_take)/gather | solution.py:140
  38.8 6.8 %gather_fusion.2 = pred[1024]{0:T(1024)(128)(4,1)S(1)} fusion(pred[1024]{0:T(1024)(128)(4,1)S(1)} %fusion.24, s32[1024]{0:T(1024)S(1)} %broadcast_clamp_fusion), kind=kCustom, calls=%fused_computation.2 | custom fusion | bytes 6144 | tf_op jit(solution)/shard_map/jit(_take)/gather | solution.py:176
  48.1 2.0 %all_gather.6 = bf16[1024,128]{1,0:T(8,128)(2,1)S(1)} all-gather(bf16[512,128]{1,0:T(8,128)(2,1)S(1)} %bitcast.72), channel_id=1, replica_groups=mesh['groups'=2,'ulysses'=8,'seq'=2] {'seq'}, dimensions={0}, use_global_device_ids=true | all-gather | bytes 393216 | tf_op jit(solution)/shard_map/all_gather | solution.py:157
  50.1 2.1 %all_gather.7 = bf16[1024,128]{1,0:T(8,128)(2,1)} all-gather(bf16[512,128]{1,0:T(8,128)(2,1)S(1)} %bitcast.73), channel_id=1, replica_groups=mesh['groups'=2,'ulysses'=8,'seq'=2] {'seq'}, dimensions={0}, use_global_device_ids=true | all-gather | bytes 393216 | tf_op jit(solution)/shard_map/all_gather | solution.py:158
  52.2 1.9 %all-to-all-done.1 = bf16[64,8,1024]{2,0,1:T(8,128)(2,1)S(1)} async-done(((bf16[64,8,1024]{2,0,1:T(8,128)(2,1)}), bf16[64,8,1024]{2,0,1:T(8,128)(2,1)S(1)}, u32[]{:S(2)}, u32[]{:S(2)}) %all-to-all-start.1) | async-done | bytes 1048608 | tf_op jit(solution)/shard_map/all_to_all | solution.py:127
  55.2 31.6 %while.31 = (s32[]{:T(128)}, f32[512,8]{0,1:T(8,128)S(1)}, f32[512,8]{0,1:T(8,128)}, f32[512,8,128]{2,0,1:T(8,128)S(1)}, s32[1024]{0:T(1024)}, /*index=5*/s32[]{...) while((s32[]{:T(128)}, f32[512,8]{0,1:T(8,128)S(1)}, ...), condition=%wide.region_8.9_spmd.clone, body=%wide.region_2.8_spmd.clone.sunk | while | flops 1098925056 | bytes 33209420 | solution.py:96
  55.2 2.0 %fusion.67 = (s32[]{:T(128)}, s32[512]{0:T(512)}) fusion(s32[1024]{0:T(1024)} %get-tuple-element.768, s32[]{:T(128)} %select_n.391), kind=kLoop, calls=%fused_computation.117.clone.1 | loop fusion | flops 511 | bytes 4104 | tf_op jit(solution)/shard_map/while/body/eval_jaxpr/while/body/eval_jaxpr/reduce_min | solution.py:79
  61.5 9.5 %conditional.3 = ((f32[512,8]{0,1:T(8,128)S(1)}, f32[512,8]{0,1:T(8,128)}, f32[512,8,128]{2,0,1:T(8,128)S(1)})) conditional(s32[]{:T(128)} %convert_element_type.25, (f32[512,8]{0,1:T(8,128)S(1)}, f32[512,8]{0,1:T(8,128)}, f32[512,8,128]{2,0,1:T(8,128)S(1)}) %tuple.76, (s32[512]{0:T(512)}, s32[512]{0:T(512)}, s32[1024]{0:T(1024)}, s32[]{:T(128)}, ...), branch_computations={%region_4.4_spmd, %region_5.7_spmd.clone} | conditional | flops 1098922496 | bytes 33194124 | solution.py:78
  66.3 1.7 %fusion.3 = f32[512,8]{0,1:T(8,128)S(1)} fusion(f32[512,512,8]{1,0,2:T(8,128)S(1)} %get-tuple-element.622, f32[512,8]{0,1:T(8,128)S(1)} %max.5, pred[512,512]{0,1:T(8,128)(4,1)S(1)} %or_and_fusion), kind=kLoop, calls=%fused_computation.7 | loop fusion | flops 8384512 | bytes 8683520 | tf_op jit(solution)/shard_map/while/body/eval_jaxpr/while/body/eval_jaxpr/cond/branch_1_fun/reduce_sum | solution.py:35
  68.1 2.8 %multiply_add_fusion = f32[512,8,128]{2,0,1:T(8,128)S(1)} fusion(f32[512,8,128]{2,0,1:T(8,128)S(1)} %get-tuple-element.554, f32[512,512,8]{1,0,2:T(8,128)S(1)} %get-tuple-element.622, f32[512,8]{0,1:T(8,128)S(1)} %max.5, pred[512,512]{0,1:T(8,128)(4,1)S(1)} %or_and_fusion, f32[512,8]{0,1:T(8,128)S(1)} %get-tuple-element.618, ...), kind=kOutput, calls=%fused_computation.11 | convolution fusion | flops 546308096 | bytes 13008900 | tf_op jit(solution)/shard_map/while/body/eval_jaxpr/while/body/eval_jaxpr/cond/branch_1_fun/qhk,kd->qhd/dot_general | solution.py:36
  71.0 2.0 %fusion.67 = (s32[]{:T(128)}, s32[512]{0:T(512)}) fusion(s32[1024]{0:T(1024)} %get-tuple-element.768, s32[]{:T(128)} %select_n.391), kind=kLoop, calls=%fused_computation.117.clone.1 | loop fusion | flops 511 | bytes 4104 | tf_op jit(solution)/shard_map/while/body/eval_jaxpr/while/body/eval_jaxpr/reduce_min | solution.py:79
  77.3 9.5 %conditional.3 = ((f32[512,8]{0,1:T(8,128)S(1)}, f32[512,8]{0,1:T(8,128)}, f32[512,8,128]{2,0,1:T(8,128)S(1)})) conditional(s32[]{:T(128)} %convert_element_type.25, (f32[512,8]{0,1:T(8,128)S(1)}, f32[512,8]{0,1:T(8,128)}, f32[512,8,128]{2,0,1:T(8,128)S(1)}) %tuple.76, (s32[512]{0:T(512)}, s32[512]{0:T(512)}, s32[1024]{0:T(1024)}, s32[]{:T(128)}, ...), branch_computations={%region_4.4_spmd, %region_5.7_spmd.clone} | conditional | flops 1098922496 | bytes 33194124 | solution.py:78
  82.1 1.7 %fusion.3 = f32[512,8]{0,1:T(8,128)S(1)} fusion(f32[512,512,8]{1,0,2:T(8,128)S(1)} %get-tuple-element.622, f32[512,8]{0,1:T(8,128)S(1)} %max.5, pred[512,512]{0,1:T(8,128)(4,1)S(1)} %or_and_fusion), kind=kLoop, calls=%fused_computation.7 | loop fusion | flops 8384512 | bytes 8683520 | tf_op jit(solution)/shard_map/while/body/eval_jaxpr/while/body/eval_jaxpr/cond/branch_1_fun/reduce_sum | solution.py:35
  83.9 2.8 %multiply_add_fusion = f32[512,8,128]{2,0,1:T(8,128)S(1)} fusion(f32[512,8,128]{2,0,1:T(8,128)S(1)} %get-tuple-element.554, f32[512,512,8]{1,0,2:T(8,128)S(1)} %get-tuple-element.622, f32[512,8]{0,1:T(8,128)S(1)} %max.5, pred[512,512]{0,1:T(8,128)(4,1)S(1)} %or_and_fusion, f32[512,8]{0,1:T(8,128)S(1)} %get-tuple-element.618, ...), kind=kOutput, calls=%fused_computation.11 | convolution fusion | flops 546308096 | bytes 13008900 | tf_op jit(solution)/shard_map/while/body/eval_jaxpr/while/body/eval_jaxpr/cond/branch_1_fun/qhk,kd->qhd/dot_general | solution.py:36
  86.8 1.9 %copy.37 = f32[512,8,128]{0,2,1:T(8,128)} copy(f32[512,8,128]{2,0,1:T(8,128)S(1)} %get-tuple-element.428) | data formatting | bytes 4194304 | tf_op jit(solution)/shard_map/while/body/eval_jaxpr/while | solution.py:96
  88.7 1.9 %divide_convert_fusion = bf16[512,8,128]{0,2,1:T(8,128)(2,1)S(1)} fusion(f32[512,8,128]{0,2,1:T(8,128)} %copy.37, f32[512,8]{0,1:T(8,128)} %get-tuple-element.429), kind=kLoop, calls=%fused_computation.36 | loop fusion | flops 1048576 | bytes 3162112 | tf_op jit(solution)/shard_map/convert_element_type | solution.py:181
  93.8 29.9 %all_to_all.60 = bf16[8,2,32768]{2,1,0:T(2,128)(2,1)S(1)} all-to-all(bf16[8,2,32768]{2,1,0:T(2,128)(2,1)S(1)} %reshape.331), channel_id=1, replica_groups=mesh['groups'=2,'ulysses'=8,'seq'=2] {'ulysses'}, dimensions={0} | all-to-all | bytes 2097152 | tf_op jit(solution)/shard_map/all_to_all | solution.py:184
  (66 shorter events, 28.3 us)
Async XLA Ops:
  0.0 0.9 copy-start
  0.0 36.2 %copy-start.1 = (s32[1024]{0:T(1024)S(1)}, s32[1024]{0:T(1024)}, u32[]{:S(2)}) copy-start(s32[1024]{0:T(1024)} %param.12) | copy-start | bytes 12292
  0.9 37.7 %copy-start.5 = (s32[128]{0:T(128)S(1)}, s32[128]{0:T(128)}, u32[]{:S(2)}) copy-start(s32[128]{0:T(128)} %param.13) | copy-start | bytes 1540
  1.6 14.6 %all-to-all-start = ((bf16[64,8,128]{2,0,1:T(8,128)(2,1)}), bf16[64,8,128]{2,0,1:T(8,128)(2,1)S(1)}, u32[]{:S(2)}, u32[]{:S(2)}) async-start(bf16[64,8,128]{2,0,1:T(8,128)(2,1)} %copy_bitcast_fusion.2), calls=%async_computation | async-start | bytes 262144 | tf_op jit(solution)/shard_map/all_to_all | solution.py:147
  16.2 10.7 %all-to-all-start.2 = ((bf16[64,8,128]{2,0,1:T(8,128)(2,1)}), bf16[64,8,128]{2,0,1:T(8,128)(2,1)S(1)}, u32[]{:S(2)}, u32[]{:S(2)}) async-start(bf16[64,8,128]{2,0,1:T(8,128)(2,1)} %copy_bitcast_fusion.1), calls=%async_computation.2 | async-start | bytes 262144 | tf_op jit(solution)/shard_map/all_to_all | solution.py:150
  26.9 27.2 %all-to-all-start.1 = ((bf16[64,8,1024]{2,0,1:T(8,128)(2,1)}), bf16[64,8,1024]{2,0,1:T(8,128)(2,1)S(1)}, u32[]{:S(2)}, u32[]{:S(2)}) async-start(bf16[64,8,1024]{2,0,1:T(8,128)(2,1)} %bitcast.66), calls=%async_computation.1 | async-start | bytes 2097152 | tf_op jit(solution)/shard_map/all_to_all | solution.py:127
  64.8 3.3 %copy-start.2 = (f32[512,8]{0,1:T(8,128)S(1)}, f32[512,8]{0,1:T(8,128)}, u32[]{:S(2)}) copy-start(f32[512,8]{0,1:T(8,128)} %get-tuple-element.553) | copy-start | bytes 49156 | tf_op jit(solution)/shard_map/while/body/eval_jaxpr/while/body/eval_jaxpr/cond
  64.8 3.3 %copy-start.4 = (bf16[1024,128]{1,0:T(8,128)(2,1)S(1)}, bf16[1024,128]{1,0:T(8,128)(2,1)}, u32[]{:S(2)}) copy-start(bf16[1024,128]{1,0:T(8,128)(2,1)} %get-tuple-element.555) | copy-start | bytes 786436 | tf_op jit(solution)/shard_map/while/body/eval_jaxpr/while/body/eval_jaxpr/cond
  68.1 2.9 %copy-start.3 = (f32[512,8]{0,1:T(8,128)}, f32[512,8]{0,1:T(8,128)S(1)}, u32[]{:S(2)}) copy-start(f32[512,8]{0,1:T(8,128)S(1)} %get-tuple-element.726) | copy-start | bytes 49156 | tf_op jit(solution)/shard_map/while/body/eval_jaxpr/while/body/eval_jaxpr/cond
  80.6 3.3 %copy-start.2 = (f32[512,8]{0,1:T(8,128)S(1)}, f32[512,8]{0,1:T(8,128)}, u32[]{:S(2)}) copy-start(f32[512,8]{0,1:T(8,128)} %get-tuple-element.553) | copy-start | bytes 49156 | tf_op jit(solution)/shard_map/while/body/eval_jaxpr/while/body/eval_jaxpr/cond
  80.6 3.3 %copy-start.4 = (bf16[1024,128]{1,0:T(8,128)(2,1)S(1)}, bf16[1024,128]{1,0:T(8,128)(2,1)}, u32[]{:S(2)}) copy-start(bf16[1024,128]{1,0:T(8,128)(2,1)} %get-tuple-element.555) | copy-start | bytes 786436 | tf_op jit(solution)/shard_map/while/body/eval_jaxpr/while/body/eval_jaxpr/cond
  83.9 2.9 %copy-start.3 = (f32[512,8]{0,1:T(8,128)}, f32[512,8]{0,1:T(8,128)S(1)}, u32[]{:S(2)}) copy-start(f32[512,8]{0,1:T(8,128)S(1)} %get-tuple-element.726) | copy-start | bytes 49156 | tf_op jit(solution)/shard_map/while/body/eval_jaxpr/while/body/eval_jaxpr/cond
where the time goes:
time: 127 us; the launch traced here: 126 us
  local copies, waits for them, and re-layouts  34.1 us (27%)
  blocking collectives  34 us (27%)
  other arithmetic  19.5 us (15%)
  starting transfers between devices  14.2 us (11%)
  waiting for transfers between devices  12.6 us (10%)
  matrix products  8.7 us (7%)
  loops' own time  2.94 us (2%)
    all_to_all x1, blocking collectives, shards(): lax.all_to_all(result, 'ulysses', split_axis=0, concat_axis=1, tiled=True)  29.9 us
    all_to_all x1, starting transfers between devices, shards(): lax.all_to_all(spread(key_states, ulysses_count), 'ulysses', split_axis=1...  7.28 us
    gather x1, local copies, waits for them, and re-layouts, shards(): jnp.take(judged, key_place)  6.8 us
    all_to_all x1, waiting for transfers between devices, shards(): lax.all_to_all(spread(key_states, ulysses_count), 'ulysses', split_axis=1...  5.76 us
    gather x1, local copies, waits for them, and re-layouts, shards(): jnp.take(turn_ids, key_place)  5.72 us
    dot_general x2, matrix products, absorb(): jnp.einsum('qhk,kd->qhd', weights.astype(jnp.bfloat16), values_block, pre...  5.69 us
    unnamed x13, local copies, waits for them, and re-layouts  5.12 us
    all_to_all x1, waiting for transfers between devices, shards(): lax.all_to_all(spread(value_states, ulysses_count), 'ulysses', split_axis...  4.99 us
  transfers between devices with their start and end apart: 3, of which 3 were waited for; matrix products, arithmetic and copies ran while one was open for 17% of the time, Pallas kernels for 0%

commit v1 on v0

--- a/solution.py
+++ b/solution.py
@@ -6,6 +6,18 @@
 
 HEAD_DIM = 128
 floor_score = -1e30
+
+
+def exchange_directly(array, axis, split, join):
+    ways, here = (lax.axis_size(axis), lax.axis_index(axis))
+    width = array.shape[split] // ways
+    turned = jnp.roll(array, -here * width, axis=split)
+    got = [lax.slice_in_dim(turned, 0, width, axis=split)]
+    for far in range(1, ways):
+        sent = lax.slice_in_dim(turned, far * width, (far + 1) * width, axis=split)
+        got.append(lax.ppermute(sent, axis, [(d, (d + far) % ways) for d in range(ways)]))
+    line = jnp.concatenate(got[::-1], axis=join)
+    return jnp.roll(line, (here + 1) * got[0].shape[join], axis=join)
 
 
 def absorb(
@@ -147,9 +159,7 @@
         lax.all_to_all(
             spread(key_states, ulysses_count), "ulysses", split_axis=1, concat_axis=0, tiled=True
         ),
-        lax.all_to_all(
-            spread(value_states, ulysses_count), "ulysses", split_axis=1, concat_axis=0, tiled=True
-        ),
+        exchange_directly(spread(value_states, ulysses_count), "ulysses", 1, 0),
     )
     key_rows = keys_out.reshape(query_total, HEAD_DIM)
     value_rows = values_out.reshape(query_total, HEAD_DIM)

time: 127 us -> 141 us (1.11)
  starting transfers between devices: 14.2 us -> 23.6 us
  waiting for transfers between devices: 12.6 us -> 18.3 us
  blocking collectives: 34 us -> 32.5 us
    all_to_all x1, waiting for transfers between devices: 1.86 us -> 17.8 us  [shards(): lax.all_to_all(query_states.reshape(tokens_here, ulysses_count, heads_her...]
    ppermute x0 -> x7, starting transfers between devices: none -> 11.2 us  [exchange_directly(): lax.ppermute(sent, axis, [(d, (d + far) % ways) for d in range(ways)])]
    all_to_all x1, waiting for transfers between devices: 5.76 us -> 0.01 us  [shards(): lax.all_to_all(spread(key_states, ulysses_count), 'ulysses', split_axis=1...]
    all_to_all x1 -> x0, waiting for transfers between devices: 4.99 us -> none  [shards(): lax.all_to_all(spread(value_states, ulysses_count), 'ulysses', split_axis...]
    all_to_all x1 -> x0, starting transfers between devices: 3.37 us -> none  [shards(): lax.all_to_all(spread(value_states, ulysses_count), 'ulysses', split_axis...]
    all_to_all x1, blocking collectives: 29.9 us -> 28.2 us  [shards(): lax.all_to_all(result, 'ulysses', split_axis=0, concat_axis=1, tiled=True)]
    unnamed x13 -> x27, local copies, waits for them, and re-layouts: 5.12 us -> 6.72 us
    another operation x2 -> x1, local copies, waits for them, and re-layouts: 2.26 us -> 0.67 us  [spread(): return widened.reshape(row_count, copies, HEAD_DIM)]
  transfers between devices with their start and end apart: 3 -> 9, of which waited for: 3 -> 2; matrix products, arithmetic and copies ran while one was open for 17% -> 16% of each run, Pallas kernels for 0% -> 0%
where the time goes in v1:
time: 141 us
  local copies, waits for them, and re-layouts  34.5 us (24%)
  blocking collectives  32.5 us (23%)
  starting transfers between devices  23.6 us (17%)
  other arithmetic  20.2 us (14%)
  waiting for transfers between devices  18.3 us (13%)
  matrix products  8.7 us (6%)
  loops' own time  2.76 us (2%)
    all_to_all x1, blocking collectives, shards(): lax.all_to_all(result, 'ulysses', split_axis=0, concat_axis=1, tiled=True)  28.2 us
    all_to_all x1, waiting for transfers between devices, shards(): lax.all_to_all(query_states.reshape(tokens_here, ulysses_count, heads_her...  17.8 us
    ppermute x7, starting transfers between devices, exchange_directly(): lax.ppermute(sent, axis, [(d, (d + far) % ways) for d in range(ways)])  11.2 us
    all_to_all x1, starting transfers between devices, shards(): lax.all_to_all(spread(key_states, ulysses_count), 'ulysses', split_axis=1...  7.28 us
    gather x1, local copies, waits for them, and re-layouts, shards(): jnp.take(judged, key_place)  6.8 us
    unnamed x27, local copies, waits for them, and re-layouts  6.72 us
    gather x1, local copies, waits for them, and re-layouts, shards(): jnp.take(turn_ids, key_place)  5.72 us
    dot_general x2, matrix products, absorb(): jnp.einsum('qhk,kd->qhd', weights.astype(jnp.bfloat16), values_block, pre...  5.68 us
  transfers between devices with their start and end apart: 9, of which 2 were waited for; matrix products, arithmetic and copies ran while one was open for 16% of the time, Pallas kernels for 0%

profile of v1, /device:TPU:0, one launch (start us, length us, event | category | flops | bytes accessed | tf_op | source)
XLA Modules:
  0.0 140.7 jit_solution(14219936591766409970)
XLA Ops:
  1.6 7.3 %all-to-all-start = ((bf16[64,8,128]{2,0,1:T(8,128)(2,1)}), bf16[64,8,128]{2,0,1:T(8,128)(2,1)S(1)}, u32[]{:S(2)}, u32[]{:S(2)}) async-start(bf16[64,8,128]{2,0,1:T(8,128)(2,1)} %copy_bitcast_fusion.1), calls=%async_computation | async-start | bytes 262144 | tf_op jit(solution)/shard_map/all_to_all | solution.py:159
  10.1 4.8 %collective-permute-start = (bf16[64,1,128]{2,1,0:T(2,128)(2,1)S(1)}, bf16[64,1,128]{2,1,0:T(2,128)(2,1)S(1)}, u32[]{:S(2)}, u32[]{:S(2)}) collective-permute-start(bf16[64,1,128]{2,1,0:T(2,128)(2,1)S(1)} %get-tuple-element.631), channel_id=1, source_target_pairs={{0,14},{2,0},{4,2},{6,4},{8,6},{10,8},{12,10},{14,12},{1,15},{3,1}... | collective-permute-start | bytes 49160 | tf_op jit(solution)/shard_map/ppermute | solution.py:18
  15.5 2.9 %collective-permute-start.3 = (bf16[64,1,128]{2,1,0:T(2,128)(2,1)S(1)}, bf16[64,1,128]{2,1,0:T(2,128)(2,1)S(1)}, u32[]{:S(2)}, u32[]{:S(2)}) collective-permute-start(bf16[64,1,128]{2,1,0:T(2,128)(2,1)S(1)} %get-tuple-element.628), channel_id=1, source_target_pairs={{0,8},{2,10},{4,12},{6,14},{8,0},{10,2},{12,4},{14,6},{1,9},{3,11}... | collective-permute-start | bytes 49160 | tf_op jit(solution)/shard_map/ppermute | solution.py:18
  18.4 5.7 %gather_fusion = s32[1024]{0:T(1024)S(1)} fusion(s32[1024]{0:T(1024)} %param.12, s32[1024]{0:T(1024)S(1)} %broadcast_clamp_fusion), kind=kCustom, calls=%fused_computation | custom fusion | bytes 12288 | tf_op jit(solution)/shard_map/jit(_take)/gather | solution.py:185
  24.8 3.4 %gather_fusion.1 = s32[512]{0:T(512)S(1)} fusion(s32[1024]{0:T(1024)} %param.12, s32[1024]{0:T(1024)S(1)} %pad_clamp_fusion), kind=kCustom, calls=%fused_computation.1 | custom fusion | bytes 6144 | tf_op jit(solution)/shard_map/jit(_take)/gather | solution.py:152
  30.3 6.8 %gather_fusion.2 = pred[1024]{0:T(1024)(128)(4,1)S(1)} fusion(pred[1024]{0:T(1024)(128)(4,1)S(1)} %fusion.24, s32[1024]{0:T(1024)S(1)} %broadcast_clamp_fusion), kind=kCustom, calls=%fused_computation.2 | custom fusion | bytes 6144 | tf_op jit(solution)/shard_map/jit(_take)/gather | solution.py:186
  38.8 2.0 %collective-permute-start.5 = (bf16[64,1,128]{2,1,0:T(2,128)(2,1)S(1)}, bf16[64,1,128]{2,1,0:T(2,128)(2,1)S(1)}, u32[]{:S(2)}, u32[]{:S(2)}) collective-permute-start(bf16[64,1,128]{2,1,0:T(2,128)(2,1)S(1)} %get-tuple-element.626), channel_id=1, source_target_pairs={{0,4},{2,6},{4,8},{6,10},{8,12},{10,14},{12,0},{14,2},{1,5},{3,7},... | collective-permute-start | bytes 49160 | tf_op jit(solution)/shard_map/ppermute | solution.py:18
  41.9 5.1 %all-to-all-start.1 = ((bf16[64,8,1024]{2,0,1:T(8,128)(2,1)}), bf16[64,8,1024]{2,0,1:T(8,128)(2,1)S(1)}, u32[]{:S(2)}, u32[]{:S(2)}) async-start(bf16[64,8,1024]{2,0,1:T(8,128)(2,1)} %bitcast.59), calls=%async_computation.1 | async-start | bytes 2097152 | tf_op jit(solution)/shard_map/all_to_all | solution.py:139
  48.4 2.1 %all-gather = bf16[1024,1,128]{2,0,1:T(8,128)(2,1)} all-gather(bf16[512,1,128]{2,0,1:T(8,128)(2,1)S(1)} %copy.32), channel_id=2, replica_groups=mesh['groups'=2,'ulysses'=8,'seq'=2] {'seq'}, dimensions={0}, use_global_device_ids=true | all-gather | bytes 393216 | tf_op jit(solution)/shard_map/all_gather | solution.py:168
  50.5 2.2 %all_gather.6 = bf16[1024,128]{1,0:T(8,128)(2,1)S(1)} all-gather(bf16[512,128]{1,0:T(8,128)(2,1)S(1)} %bitcast.65), channel_id=1, replica_groups=mesh['groups'=2,'ulysses'=8,'seq'=2] {'seq'}, dimensions={0}, use_global_device_ids=true | all-gather | bytes 393216 | tf_op jit(solution)/shard_map/all_gather | solution.py:167
  52.7 17.8 %all-to-all-done.1 = bf16[64,8,1024]{2,0,1:T(8,128)(2,1)S(1)} async-done(((bf16[64,8,1024]{2,0,1:T(8,128)(2,1)}), bf16[64,8,1024]{2,0,1:T(8,128)(2,1)S(1)}, u32[]{:S(2)}, u32[]{:S(2)}) %all-to-all-start.1) | async-done | bytes 1048608 | tf_op jit(solution)/shard_map/all_to_all | solution.py:139
  71.7 31.3 %while.31 = (s32[]{:T(128)}, f32[512,8]{0,1:T(8,128)S(1)}, f32[512,8]{0,1:T(8,128)}, f32[512,8,128]{2,0,1:T(8,128)S(1)}, s32[1024]{0:T(1024)}, /*index=5*/s32[]{...) while((s32[]{:T(128)}, f32[512,8]{0,1:T(8,128)S(1)}, ...), condition=%wide.region_8.9_spmd.clone, body=%wide.region_2.8_spmd.clone.sunk | while | flops 1098925056 | bytes 33209420 | solution.py:108
  71.7 2.0 %fusion.68 = (s32[]{:T(128)}, s32[512]{0:T(512)}) fusion(s32[1024]{0:T(1024)} %get-tuple-element.775, s32[]{:T(128)} %select_n.417), kind=kLoop, calls=%fused_computation.136.clone.1 | loop fusion | flops 511 | bytes 4104 | tf_op jit(solution)/shard_map/while/body/eval_jaxpr/while/body/eval_jaxpr/reduce_min | solution.py:91
  77.8 9.5 %conditional.3 = ((f32[512,8]{0,1:T(8,128)S(1)}, f32[512,8]{0,1:T(8,128)}, f32[512,8,128]{2,0,1:T(8,128)S(1)})) conditional(s32[]{:T(128)} %convert_element_type.25, (f32[512,8]{0,1:T(8,128)S(1)}, f32[512,8]{0,1:T(8,128)}, f32[512,8,128]{2,0,1:T(8,128)S(1)}) %tuple.82, (s32[512]{0:T(512)}, s32[512]{0:T(512)}, s32[1024]{0:T(1024)}, s32[]{:T(128)}, ...), branch_computations={%region_4.4_spmd, %region_5.7_spmd.clone} | conditional | flops 1098922496 | bytes 33194124 | solution.py:90
  81.1 1.5 %fusion.4 = (f32[512,8]{0,1:T(8,128)S(1)}, f32[512,512,8]{1,0,2:T(8,128)S(1)}) fusion(pred[512,512]{0,1:T(8,128)(4,1)S(1)} %or_and_fusion, bf16[512,8,128]{2,0,1:T(8,128)(2,1)S(1)} %get-tuple-element.552, bf16[1024,128]{1,0:T(8,128)(2,1)S(1)} %get-tuple-element.551, s32[]{:T(128)} %get-tuple-element.548), kind=kOutput, calls=%fused_computation.8 | convolution fusion | flops 543158272 | bytes 9846788 | tf_op jit(solution)/shard_map/while/body/eval_jaxpr/while/body/eval_jaxpr/cond/branch_1_fun/qhd,kd->qhk/dot_general | solution.py:37
  82.6 1.7 %fusion.3 = f32[512,8]{0,1:T(8,128)S(1)} fusion(f32[512,512,8]{1,0,2:T(8,128)S(1)} %get-tuple-element.622, f32[512,8]{0,1:T(8,128)S(1)} %max.5, pred[512,512]{0,1:T(8,128)(4,1)S(1)} %or_and_fusion), kind=kLoop, calls=%fused_computation.7 | loop fusion | flops 8384512 | bytes 8683520 | tf_op jit(solution)/shard_map/while/body/eval_jaxpr/while/body/eval_jaxpr/cond/branch_1_fun/reduce_sum | solution.py:47
  84.4 2.8 %multiply_add_fusion = f32[512,8,128]{2,0,1:T(8,128)S(1)} fusion(f32[512,8,128]{2,0,1:T(8,128)S(1)} %get-tuple-element.554, f32[512,512,8]{1,0,2:T(8,128)S(1)} %get-tuple-element.622, f32[512,8]{0,1:T(8,128)S(1)} %max.5, pred[512,512]{0,1:T(8,128)(4,1)S(1)} %or_and_fusion, f32[512,8]{0,1:T(8,128)S(1)} %get-tuple-element.618, ...), kind=kOutput, calls=%fused_computation.11 | convolution fusion | flops 546308096 | bytes 13008900 | tf_op jit(solution)/shard_map/while/body/eval_jaxpr/while/body/eval_jaxpr/cond/branch_1_fun/qhk,kd->qhd/dot_general | solution.py:48
  87.3 2.0 %fusion.68 = (s32[]{:T(128)}, s32[512]{0:T(512)}) fusion(s32[1024]{0:T(1024)} %get-tuple-element.775, s32[]{:T(128)} %select_n.417), kind=kLoop, calls=%fused_computation.136.clone.1 | loop fusion | flops 511 | bytes 4104 | tf_op jit(solution)/shard_map/while/body/eval_jaxpr/while/body/eval_jaxpr/reduce_min | solution.py:91
  93.4 9.5 %conditional.3 = ((f32[512,8]{0,1:T(8,128)S(1)}, f32[512,8]{0,1:T(8,128)}, f32[512,8,128]{2,0,1:T(8,128)S(1)})) conditional(s32[]{:T(128)} %convert_element_type.25, (f32[512,8]{0,1:T(8,128)S(1)}, f32[512,8]{0,1:T(8,128)}, f32[512,8,128]{2,0,1:T(8,128)S(1)}) %tuple.82, (s32[512]{0:T(512)}, s32[512]{0:T(512)}, s32[1024]{0:T(1024)}, s32[]{:T(128)}, ...), branch_computations={%region_4.4_spmd, %region_5.7_spmd.clone} | conditional | flops 1098922496 | bytes 33194124 | solution.py:90
  98.3 1.7 %fusion.3 = f32[512,8]{0,1:T(8,128)S(1)} fusion(f32[512,512,8]{1,0,2:T(8,128)S(1)} %get-tuple-element.622, f32[512,8]{0,1:T(8,128)S(1)} %max.5, pred[512,512]{0,1:T(8,128)(4,1)S(1)} %or_and_fusion), kind=kLoop, calls=%fused_computation.7 | loop fusion | flops 8384512 | bytes 8683520 | tf_op jit(solution)/shard_map/while/body/eval_jaxpr/while/body/eval_jaxpr/cond/branch_1_fun/reduce_sum | solution.py:47
  100.1 2.8 %multiply_add_fusion = f32[512,8,128]{2,0,1:T(8,128)S(1)} fusion(f32[512,8,128]{2,0,1:T(8,128)S(1)} %get-tuple-element.554, f32[512,512,8]{1,0,2:T(8,128)S(1)} %get-tuple-element.622, f32[512,8]{0,1:T(8,128)S(1)} %max.5, pred[512,512]{0,1:T(8,128)(4,1)S(1)} %or_and_fusion, f32[512,8]{0,1:T(8,128)S(1)} %get-tuple-element.618, ...), kind=kOutput, calls=%fused_computation.11 | convolution fusion | flops 546308096 | bytes 13008900 | tf_op jit(solution)/shard_map/while/body/eval_jaxpr/while/body/eval_jaxpr/cond/branch_1_fun/qhk,kd->qhd/dot_general | solution.py:48
  103.0 1.9 %copy.34 = f32[512,8,128]{0,2,1:T(8,128)} copy(f32[512,8,128]{2,0,1:T(8,128)S(1)} %get-tuple-element.428) | data formatting | bytes 4194304 | tf_op jit(solution)/shard_map/while/body/eval_jaxpr/while | solution.py:108
  104.8 1.9 %divide_convert_fusion = bf16[512,8,128]{0,2,1:T(8,128)(2,1)S(1)} fusion(f32[512,8,128]{0,2,1:T(8,128)} %copy.34, f32[512,8]{0,1:T(8,128)} %get-tuple-element.429), kind=kLoop, calls=%fused_computation.36 | loop fusion | flops 1048576 | bytes 3162112 | tf_op jit(solution)/shard_map/convert_element_type | solution.py:191
  110.0 28.2 %all_to_all.45 = bf16[8,2,32768]{2,1,0:T(2,128)(2,1)S(1)} all-to-all(bf16[8,2,32768]{2,1,0:T(2,128)(2,1)S(1)} %reshape.331), channel_id=1, replica_groups=mesh['groups'=2,'ulysses'=8,'seq'=2] {'ulysses'}, dimensions={0} | all-to-all | bytes 2097152 | tf_op jit(solution)/shard_map/all_to_all | solution.py:194
  (96 shorter events, 31.1 us)
Async XLA Ops:
  0.0 0.9 copy-start
  0.9 36.8 %copy-start.1 = (bf16[64,8192]{1,0:T(8,128)(2,1)S(1)}, bf16[64,8192]{1,0:T(8,128)(2,1)}, u32[]{:S(2)}) copy-start(bf16[64,8192]{1,0:T(8,128)(2,1)} %param.9) | copy-start | bytes 3145732
  1.6 40.3 %all-to-all-start = ((bf16[64,8,128]{2,0,1:T(8,128)(2,1)}), bf16[64,8,128]{2,0,1:T(8,128)(2,1)S(1)}, u32[]{:S(2)}, u32[]{:S(2)}) async-start(bf16[64,8,128]{2,0,1:T(8,128)(2,1)} %copy_bitcast_fusion.1), calls=%async_computation | async-start | bytes 262144 | tf_op jit(solution)/shard_map/all_to_all | solution.py:159
  10.1 28.7 %collective-permute-start = (bf16[64,1,128]{2,1,0:T(2,128)(2,1)S(1)}, bf16[64,1,128]{2,1,0:T(2,128)(2,1)S(1)}, u32[]{:S(2)}, u32[]{:S(2)}) collective-permute-start(bf16[64,1,128]{2,1,0:T(2,128)(2,1)S(1)} %get-tuple-element.631), channel_id=1, source_target_pairs={{0,14},{2,0},{4,2},{6,4},{8,6},{10,8},{12,10},{14,12},{1,15},{3,1}... | collective-permute-start | bytes 49160 | tf_op jit(solution)/shard_map/ppermute | solution.py:18
  14.9 25.9 %collective-permute-start.1 = (bf16[64,1,128]{2,1,0:T(2,128)(2,1)S(1)}, bf16[64,1,128]{2,1,0:T(2,128)(2,1)S(1)}, u32[]{:S(2)}, u32[]{:S(2)}) collective-permute-start(bf16[64,1,128]{2,1,0:T(2,128)(2,1)S(1)} %get-tuple-element.630), channel_id=1, source_target_pairs={{0,12},{2,14},{4,0},{6,2},{8,4},{10,6},{12,8},{14,10},{1,13},{3,15... | collective-permute-start | bytes 49160 | tf_op jit(solution)/shard_map/ppermute | solution.py:18
  15.5 26.4 %collective-permute-start.2 = (bf16[64,1,128]{2,1,0:T(2,128)(2,1)S(1)}, bf16[64,1,128]{2,1,0:T(2,128)(2,1)S(1)}, u32[]{:S(2)}, u32[]{:S(2)}) collective-permute-start(bf16[64,1,128]{2,1,0:T(2,128)(2,1)S(1)} %get-tuple-element.629), channel_id=1, source_target_pairs={{0,10},{2,12},{4,14},{6,0},{8,2},{10,4},{12,6},{14,8},{1,11},{3,13... | collective-permute-start | bytes 49160 | tf_op jit(solution)/shard_map/ppermute | solution.py:18
  15.5 31.6 %collective-permute-start.3 = (bf16[64,1,128]{2,1,0:T(2,128)(2,1)S(1)}, bf16[64,1,128]{2,1,0:T(2,128)(2,1)S(1)}, u32[]{:S(2)}, u32[]{:S(2)}) collective-permute-start(bf16[64,1,128]{2,1,0:T(2,128)(2,1)S(1)} %get-tuple-element.628), channel_id=1, source_target_pairs={{0,8},{2,10},{4,12},{6,14},{8,0},{10,2},{12,4},{14,6},{1,9},{3,11}... | collective-permute-start | bytes 49160 | tf_op jit(solution)/shard_map/ppermute | solution.py:18
  18.4 28.7 %collective-permute-start.4 = (bf16[64,1,128]{2,1,0:T(2,128)(2,1)S(1)}, bf16[64,1,128]{2,1,0:T(2,128)(2,1)S(1)}, u32[]{:S(2)}, u32[]{:S(2)}) collective-permute-start(bf16[64,1,128]{2,1,0:T(2,128)(2,1)S(1)} %get-tuple-element.627), channel_id=1, source_target_pairs={{0,6},{2,8},{4,10},{6,12},{8,14},{10,0},{12,2},{14,4},{1,7},{3,9},... | collective-permute-start | bytes 49160 | tf_op jit(solution)/shard_map/ppermute | solution.py:18
  38.8 8.4 %collective-permute-start.5 = (bf16[64,1,128]{2,1,0:T(2,128)(2,1)S(1)}, bf16[64,1,128]{2,1,0:T(2,128)(2,1)S(1)}, u32[]{:S(2)}, u32[]{:S(2)}) collective-permute-start(bf16[64,1,128]{2,1,0:T(2,128)(2,1)S(1)} %get-tuple-element.626), channel_id=1, source_target_pairs={{0,4},{2,6},{4,8},{6,10},{8,12},{10,14},{12,0},{14,2},{1,5},{3,7},... | collective-permute-start | bytes 49160 | tf_op jit(solution)/shard_map/ppermute | solution.py:18
  40.8 6.8 %collective-permute-start.6 = (bf16[64,1,128]{2,1,0:T(2,128)(2,1)S(1)}, bf16[64,1,128]{2,1,0:T(2,128)(2,1)S(1)}, u32[]{:S(2)}, u32[]{:S(2)}) collective-permute-start(bf16[64,1,128]{2,1,0:T(2,128)(2,1)S(1)} %get-tuple-element.625), channel_id=1, source_target_pairs={{0,2},{2,4},{4,6},{6,8},{8,10},{10,12},{12,14},{14,0},{1,3},{3,5},... | collective-permute-start | bytes 49160 | tf_op jit(solution)/shard_map/ppermute | solution.py:18
  41.9 28.6 %all-to-all-start.1 = ((bf16[64,8,1024]{2,0,1:T(8,128)(2,1)}), bf16[64,8,1024]{2,0,1:T(8,128)(2,1)S(1)}, u32[]{:S(2)}, u32[]{:S(2)}) async-start(bf16[64,8,1024]{2,0,1:T(8,128)(2,1)} %bitcast.59), calls=%async_computation.1 | async-start | bytes 2097152 | tf_op jit(solution)/shard_map/all_to_all | solution.py:139
  81.1 3.3 %copy-start.2 = (f32[512,8]{0,1:T(8,128)S(1)}, f32[512,8]{0,1:T(8,128)}, u32[]{:S(2)}) copy-start(f32[512,8]{0,1:T(8,128)} %get-tuple-element.553) | copy-start | bytes 49156 | tf_op jit(solution)/shard_map/while/body/eval_jaxpr/while/body/eval_jaxpr/cond
  81.1 3.3 %copy-start.4 = (bf16[1024,128]{1,0:T(8,128)(2,1)S(1)}, bf16[1024,128]{1,0:T(8,128)(2,1)}, u32[]{:S(2)}) copy-start(bf16[1024,128]{1,0:T(8,128)(2,1)} %get-tuple-element.555) | copy-start | bytes 786436 | tf_op jit(solution)/shard_map/while/body/eval_jaxpr/while/body/eval_jaxpr/cond
  84.4 2.9 %copy-start.3 = (f32[512,8]{0,1:T(8,128)}, f32[512,8]{0,1:T(8,128)S(1)}, u32[]{:S(2)}) copy-start(f32[512,8]{0,1:T(8,128)S(1)} %get-tuple-element.733) | copy-start | bytes 49156 | tf_op jit(solution)/shard_map/while/body/eval_jaxpr/while/body/eval_jaxpr/cond
  96.7 3.3 %copy-start.2 = (f32[512,8]{0,1:T(8,128)S(1)}, f32[512,8]{0,1:T(8,128)}, u32[]{:S(2)}) copy-start(f32[512,8]{0,1:T(8,128)} %get-tuple-element.553) | copy-start | bytes 49156 | tf_op jit(solution)/shard_map/while/body/eval_jaxpr/while/body/eval_jaxpr/cond
  96.7 3.3 %copy-start.4 = (bf16[1024,128]{1,0:T(8,128)(2,1)S(1)}, bf16[1024,128]{1,0:T(8,128)(2,1)}, u32[]{:S(2)}) copy-start(bf16[1024,128]{1,0:T(8,128)(2,1)} %get-tuple-element.555) | copy-start | bytes 786436 | tf_op jit(solution)/shard_map/while/body/eval_jaxpr/while/body/eval_jaxpr/cond
  100.1 2.9 %copy-start.3 = (f32[512,8]{0,1:T(8,128)}, f32[512,8]{0,1:T(8,128)S(1)}, u32[]{:S(2)}) copy-start(f32[512,8]{0,1:T(8,128)S(1)} %get-tuple-element.733) | copy-start | bytes 49156 | tf_op jit(solution)/shard_map/while/body/eval_jaxpr/while/body/eval_jaxpr/cond
